TPU v7x, 128 devices: a whole 4x4x4 slice. The times are simulated.
128 devices in a mesh: px: 8 (over y, core), py: 16 (over x, z).
Axes of the slice: x: 4, y: 4, z: 4, core: 2. Of those that a mesh axis runs over, the one named last changes fastest.
Arguments:
- control_start: float32 [2, 16, 128, 2048], P(None, 'py', None, 'px'), may hold values from -12 to 12
- coef_x: float32 [16, 128, 2048], P('py', None, 'px'), may hold values from 0.1 to 0.45
- coef_y: float32 [16, 128, 2048], P('py', 'px'), may hold values from 0.1 to 0.45
- innovation: float32 [131072, 128], P(('px', 'py')), may hold values from -6 to 6
- obs_weight: float32 [131072, 128], P(('px', 'py')), may hold values from 0.25 to 4
- interp: float32 [131072], P(('px', 'py')), may hold values from 0 to 1
- obs_owner: int32 [131072, 1], P(('px', 'py')), may hold values from 0 to 15; in each aligned block of 1024 rows (0 to 1023, 1024 to 2047, ...) at most 192 rows name the same one
- cell_key: int32 [131072], P(('px', 'py')), may hold values from 0 to 31
- stencil: int32 [131072], P(('px', 'py')), may hold values from 0 to 14
Outputs:
- control: float32 [2, 16, 128, 2048], P(None, 'py', None, 'px')
- residual: float32 [2, 16, 128, 2048], P(None, 'py', None, 'px')
Inputs may be any that keep to these rules, and one draw needn't show every extreme that they name: `obs_owner`: at most 192 of the observation rows of one device name the same owner, and exactly 192 do for some owner on some device.
All inputs are finite; a program needn't handle non-finite values.
Results may differ from a plain program's by a relative error of at most 0.00023.
Values sent between devices are 32-bit elements; how exact they have to be, the bound alone decides.
A program may use at most 64 MiB of HBM per device.

v0:
```python
import jax
import jax.numpy as jnp
from jax import lax
from jax.sharding import PartitionSpec as P

F = 2
SEG = 128
M = 4
ITERS = 2
LZ = 1
LX = 16
NB = 16


def diffuse(values, coeffs, axis_dim):
    length = values.shape[axis_dim]
    face_coef = lax.slice_in_dim(coeffs[None], 0, length - 1, axis=axis_dim)
    pad_after = [(0, 0)] * values.ndim
    pad_before = [(0, 0)] * values.ndim
    pad_after[axis_dim] = (0, 1)
    pad_before[axis_dim] = (1, 0)
    for repeat in range(M):
        next_cell = lax.slice_in_dim(values, 1, length, axis=axis_dim)
        this_cell = lax.slice_in_dim(values, 0, length - 1, axis=axis_dim)
        flux_face = face_coef * (next_cell - this_cell)
        values = values + jnp.pad(flux_face, pad_after) - jnp.pad(flux_face, pad_before)
    return values


def build_interp(shares_in, rows_in, row_count):
    row_ids = jnp.arange(row_count, dtype=jnp.int32)[None, :]
    lower_hit = (rows_in[:, None] == row_ids).astype(jnp.float32)
    upper_hit = (rows_in[:, None] + NB == row_ids).astype(jnp.float32)
    shares = shares_in[:, None]
    return (1.0 - shares) * lower_hit + shares * upper_hit


def misfit(state_in, observed, weights, interp_matrix):
    flat_field = state_in.reshape(-1, SEG)
    modelled = jnp.dot(
        interp_matrix,
        flat_field,
        precision=lax.Precision.HIGHEST,
        preferred_element_type=jnp.float32,
    )
    weighted = weights * (observed - modelled)
    result = lax.dot_general(
        interp_matrix,
        weighted,
        (((0,), (0,)), ((), ())),
        precision=lax.Precision.HIGHEST,
        preferred_element_type=jnp.float32,
    )
    return result.reshape(state_in.shape)


def dot_total(left_side, right_side):
    return lax.psum(jnp.sum(left_side * right_side), ("px", "py"))


def shards(
    control_start, coef_x, coef_y, innovation, obs_weight, interp, obs_owner, cell_key, stencil
):
    groups = lax.axis_size("py")
    capacity = 3 * innovation.shape[0] // groups
    coef_x = coef_x.at[:, -1, :].set(0.0)
    coef_y = coef_y.at[:, :, -1].set(0.0)
    field_id = cell_key // (LZ * NB)
    level_local = cell_key // NB % LZ
    row_index = ((field_id * LZ + level_local) * LX + stencil) * NB + cell_key % NB
    targets = obs_owner[:, 0]
    onehot = (targets[:, None] == jnp.arange(groups, dtype=jnp.int32)[None, :]).astype(jnp.int32)
    earlier = jnp.cumsum(onehot, axis=0) - onehot
    slot_index = jnp.sum(earlier * onehot, axis=1)
    slot_target = targets * capacity + slot_index
    total_slots = groups * capacity

    def bucket(values_in):
        buf_shape = (total_slots,) + values_in.shape[1:]
        return jnp.zeros(buf_shape, values_in.dtype).at[slot_target].set(values_in)

    arrived = (
        lax.all_to_all(bucket(innovation), "py", split_axis=0, concat_axis=0, tiled=True),
        lax.all_to_all(bucket(obs_weight), "py", split_axis=0, concat_axis=0, tiled=True),
        lax.all_to_all(bucket(interp), "py", split_axis=0, concat_axis=0, tiled=True),
        lax.all_to_all(bucket(row_index), "py", split_axis=0, concat_axis=0, tiled=True),
    )
    observed, weights, shares_in, rows_in = arrived
    interp_matrix = build_interp(shares_in, rows_in, F * LZ * LX * NB)

    def forward(values_in):
        turned = lax.all_to_all(
            diffuse(values_in, coef_x, 2), "px", split_axis=2, concat_axis=3, tiled=True
        )
        return diffuse(turned, coef_y, 3)

    def adjoint(values_in):
        turned = lax.all_to_all(
            diffuse(values_in, coef_y, 3), "px", split_axis=3, concat_axis=2, tiled=True
        )
        return diffuse(turned, coef_x, 2)

    no_data = jnp.zeros_like(observed)
    residual = (
        adjoint(misfit(forward(control_start), observed, weights, interp_matrix)) - control_start
    )
    control = control_start
    direction = residual
    norm_now = dot_total(residual, residual)
    for repeat in range(ITERS):
        applied = direction - adjoint(misfit(forward(direction), no_data, weights, interp_matrix))
        step_size = norm_now / dot_total(direction, applied)
        control = control + step_size * direction
        residual = residual - step_size * applied
        norm_next = dot_total(residual, residual)
        direction = residual + norm_next / norm_now * direction
        norm_now = norm_next
    return (control, residual)


def solution(mesh):
    return jax.shard_map(
        shards,
        mesh=mesh,
        in_specs=(
            P(None, "py", None, "px"),
            P("py", None, "px"),
            P("py", "px", None),
            P(("px", "py"), None),
            P(("px", "py"), None),
            P(("px", "py")),
            P(("px", "py"), None),
            P(("px", "py")),
            P(("px", "py")),
        ),
        out_specs=(P(None, "py", None, "px"), P(None, "py", None, "px")),
        check_vma=False,
    )
```

profile of v0, /device:TPU:1, one launch (start us, length us, event | category | flops | bytes accessed | tf_op | source)
XLA Modules:
  0.0 462.8 jit_solution(5884328285071608332)
XLA Ops:
  13.5 8.4 %all-to-all-start = ((s32[16,192,1]{1,2,0:T(1,128)}), s32[16,192,1]{1,2,0:T(1,128)S(1)}, u32[]{:S(2)}, u32[]{:S(2)}) async-start(s32[16,192,1]{1,2,0:T(1,128)} %all_to_all.143), calls=%async_computation | async-start | bytes 32768 | tf_op jit(solution)/shard_map/all_to_all | solution.py:86
  30.0 6.7 %all-to-all-start.1 = ((f32[16,192,1]{1,2,0:T(1,128)}), f32[16,192,1]{1,2,0:T(1,128)S(1)}, u32[]{:S(2)}, u32[]{:S(2)}) async-start(f32[16,192,1]{1,2,0:T(1,128)} %all_to_all.144), calls=%async_computation.1 | async-start | bytes 32768 | tf_op jit(solution)/shard_map/all_to_all | solution.py:85
  36.8 4.7 %scatter_custom_fusion.2 = f32[3072,128]{1,0:T(8,128)} fusion(s32[1024]{0:T(1024)S(1)} %bitcast.132, f32[1024,128]{1,0:T(8,128)} %param.17, f32[]{:T(128)} %constant.119.clone.1), kind=kCustom, calls=%fused_computation.51 | custom fusion | bytes 1573376 | tf_op jit(solution)/shard_map/scatter | solution.py:80
  41.5 4.7 %scatter_custom_fusion.3 = f32[3072,128]{1,0:T(8,128)} fusion(s32[1024]{0:T(1024)S(1)} %bitcast.133, f32[1024,128]{1,0:T(8,128)} %param.16, f32[]{:T(128)} %constant.119.clone.1), kind=kCustom, calls=%fused_computation.49 | custom fusion | bytes 1573376 | tf_op jit(solution)/shard_map/scatter | solution.py:80
  47.2 6.0 %all-to-all-start.4 = ((f32[2,1,128,256]{3,0,1,2:T(2,128)}), f32[2,1,128,256]{3,0,1,2:T(2,128)S(1)}, u32[]{:S(2)}, u32[]{:S(2)}) async-start(f32[2,1,128,256]{3,0,1,2:T(2,128)} %copy.120), calls=%async_computation.4 | async-start | bytes 524288 | tf_op jit(solution)/shard_map/all_to_all | solution.py:92
  53.3 6.4 %all-to-all-done.4 = f32[2,1,128,256]{3,0,1,2:T(2,128)S(1)} async-done(((f32[2,1,128,256]{3,0,1,2:T(2,128)}), f32[2,1,128,256]{3,0,1,2:T(2,128)S(1)}, u32[]{:S(2)}, u32[]{:S(2)}) %all-to-all-start.4) | async-done | bytes 262176 | tf_op jit(solution)/shard_map/all_to_all | solution.py:92
  59.6 6.9 %all-to-all-start.2 = ((f32[16,192,128]{2,1,0:T(8,128)}), f32[16,192,128]{2,1,0:T(8,128)S(1)}, u32[]{:S(2)}, u32[]{:S(2)}) async-start(f32[16,192,128]{2,1,0:T(8,128)} %bitcast.7), calls=%async_computation.2 | async-start | bytes 3145728 | tf_op jit(solution)/shard_map/all_to_all | solution.py:84
  67.2 19.9 %all-to-all-done.2 = f32[16,192,128]{2,1,0:T(8,128)S(1)} async-done(((f32[16,192,128]{2,1,0:T(8,128)}), f32[16,192,128]{2,1,0:T(8,128)S(1)}, u32[]{:S(2)}, u32[]{:S(2)}) %all-to-all-start.2) | async-done | bytes 1572896 | tf_op jit(solution)/shard_map/all_to_all | solution.py:84
  87.1 4.7 %all-to-all-start.3 = ((f32[16,192,128]{2,1,0:T(8,128)}), f32[16,192,128]{2,1,0:T(8,128)}, u32[]{:S(2)}, u32[]{:S(2)}) async-start(f32[16,192,128]{2,1,0:T(8,128)} %bitcast.9), calls=%async_computation.3 | async-start | bytes 3145728 | tf_op jit(solution)/shard_map/all_to_all | solution.py:83
  92.4 18.5 %all-to-all-done.3 = f32[16,192,128]{2,1,0:T(8,128)} async-done(((f32[16,192,128]{2,1,0:T(8,128)}), f32[16,192,128]{2,1,0:T(8,128)}, u32[]{:S(2)}, u32[]{:S(2)}) %all-to-all-start.3) | async-done | bytes 1572896 | tf_op jit(solution)/shard_map/all_to_all | solution.py:83
  111.0 9.5 %fusion.11 = f32[3072,128]{1,0:T(8,128)S(1)} fusion(f32[3072,128]{1,0:T(8,128)S(1)} %bitcast.117, f32[3072,128]{1,0:T(8,128)} %bitcast.10, f32[512,128]{1,0:T(8,128)S(1)} %reshape.123, f32[3072]{0:T(1024)S(1)} %all_to_all.112, s32[3072]{0:T(1024)S(1)} %broadcast_add_fusion.1, f32[3072]{0:T(1024)S(1)} %broadcast_subtract_fusion, s32[3072]{0:T(1024)S(1)} %eq.64), kind=kOutput, calls=%fused_computation.18 | convolution fusion | flops 2424569856 | bytes 5029888 | tf_op jit(solution)/shard_map/dot_general | solution.py:40
  120.5 11.8 %fusion.4 = f32[512,128]{1,0:T(8,128)S(1)} fusion(f32[3072,128]{1,0:T(8,128)S(1)} %fusion.11, f32[3072]{0:T(1024)S(1)} %all_to_all.112, s32[3072]{0:T(1024)S(1)} %broadcast_add_fusion.1, f32[3072]{0:T(1024)S(1)} %broadcast_subtract_fusion, s32[3072]{0:T(1024)S(1)} %eq.64), kind=kOutput, calls=%fused_computation.10 | convolution fusion | flops 2423783424 | bytes 1884160 | tf_op jit(solution)/shard_map/dot_general | solution.py:47
  137.6 14.4 %all_to_all.155 = f32[8,1,8192]{2,1,0:T(1,128)S(1)} all-to-all(f32[8,1,8192]{2,1,0:T(1,128)S(1)} %reshape.171), channel_id=1, replica_groups=mesh['px'=8,'py'=16] {'px'}, dimensions={0} | all-to-all | bytes 524288 | tf_op jit(solution)/shard_map/all_to_all | solution.py:98
  158.4 9.9 %all_to_all.156 = f32[2,1,128,256]{3,0,1,2:T(2,128)S(1)} all-to-all(f32[2,1,128,256]{3,0,1,2:T(2,128)S(1)} %copy.127), channel_id=1, replica_groups=mesh['px'=8,'py'=16] {'px'}, dimensions={2} | all-to-all | bytes 524288 | tf_op jit(solution)/shard_map/all_to_all | solution.py:92
  170.3 9.1 %fusion.10 = f32[3072,128]{1,0:T(8,128)S(1)} fusion(f32[3072,128]{1,0:T(8,128)S(1)} %bitcast.118, f32[512,128]{1,0:T(8,128)S(1)} %reshape.125, f32[3072]{0:T(1024)S(1)} %all_to_all.112, s32[3072]{0:T(1024)S(1)} %broadcast_add_fusion.1, f32[3072]{0:T(1024)S(1)} %broadcast_subtract_fusion, s32[3072]{0:T(1024)S(1)} %eq.64), kind=kOutput, calls=%fused_computation.17 | convolution fusion | flops 2424569856 | bytes 3457024 | tf_op jit(solution)/shard_map/dot_general | solution.py:40
  179.5 11.8 %fusion.2 = f32[512,128]{1,0:T(8,128)S(1)} fusion(f32[3072,128]{1,0:T(8,128)S(1)} %fusion.10, f32[3072]{0:T(1024)S(1)} %all_to_all.112, s32[3072]{0:T(1024)S(1)} %broadcast_add_fusion.1, f32[3072]{0:T(1024)S(1)} %broadcast_subtract_fusion, s32[3072]{0:T(1024)S(1)} %eq.64), kind=kOutput, calls=%fused_computation.8 | convolution fusion | flops 2423783424 | bytes 1884160 | tf_op jit(solution)/shard_map/dot_general | solution.py:47
  196.8 9.9 %all_to_all.157 = f32[8,1,8192]{2,1,0:T(1,128)S(1)} all-to-all(f32[8,1,8192]{2,1,0:T(1,128)S(1)} %reshape.173), channel_id=1, replica_groups=mesh['px'=8,'py'=16] {'px'}, dimensions={0} | all-to-all | bytes 524288 | tf_op jit(solution)/shard_map/all_to_all | solution.py:98
  212.7 63.0 %all-reduce.96 = (f32[]{:T(128)}, f32[]{:T(128)}) all-reduce(f32[]{:T(128)} %get-tuple-element.35, f32[]{:T(128)} %get-tuple-element.34), channel_id=1, replica_groups=mesh['px'=8,'py'=16] {'px','py'}, use_global_device_ids=true, to_apply=%region_8.9 | all-reduce | flops 2 | bytes 16 | tf_op jit(solution)/shard_map/psum | solution.py:58
  277.7 62.5 %psum.30 = f32[]{:T(128)} all-reduce(f32[]{:T(128)} %get-tuple-element.38), channel_id=1, replica_groups=mesh['px'=8,'py'=16] {'px','py'}, use_global_device_ids=true, to_apply=%region_12.13 | all-reduce | flops 1 | bytes 8 | tf_op jit(solution)/shard_map/psum | solution.py:58
  342.1 11.0 %all_to_all.158 = f32[2,1,128,256]{3,0,1,2:T(2,128)S(1)} all-to-all(f32[2,1,128,256]{3,0,1,2:T(2,128)S(1)} %copy.134), channel_id=1, replica_groups=mesh['px'=8,'py'=16] {'px'}, dimensions={2} | all-to-all | bytes 524288 | tf_op jit(solution)/shard_map/all_to_all | solution.py:92
  355.1 9.1 %fusion.9 = f32[3072,128]{1,0:T(8,128)S(1)} fusion(f32[3072,128]{1,0:T(8,128)S(1)} %bitcast.119, f32[512,128]{1,0:T(8,128)S(1)} %reshape.127, f32[3072]{0:T(1024)S(1)} %all_to_all.112, s32[3072]{0:T(1024)S(1)} %broadcast_add_fusion.1, f32[3072]{0:T(1024)S(1)} %broadcast_subtract_fusion, s32[3072]{0:T(1024)S(1)} %eq.64), kind=kOutput, calls=%fused_computation.16 | convolution fusion | flops 2424569856 | bytes 3457024 | tf_op jit(solution)/shard_map/dot_general | solution.py:40
  364.2 11.8 %fusion = f32[512,128]{1,0:T(8,128)S(1)} fusion(f32[3072,128]{1,0:T(8,128)S(1)} %fusion.9, f32[3072]{0:T(1024)S(1)} %all_to_all.112, s32[3072]{0:T(1024)S(1)} %broadcast_add_fusion.1, f32[3072]{0:T(1024)S(1)} %broadcast_subtract_fusion, s32[3072]{0:T(1024)S(1)} %eq.64), kind=kOutput, calls=%fused_computation.6 | convolution fusion | flops 2423783424 | bytes 1884160 | tf_op jit(solution)/shard_map/dot_general | solution.py:47
  381.3 9.9 %all_to_all.159 = f32[8,1,8192]{2,1,0:T(1,128)S(1)} all-to-all(f32[8,1,8192]{2,1,0:T(1,128)S(1)} %reshape.175), channel_id=1, replica_groups=mesh['px'=8,'py'=16] {'px'}, dimensions={0} | all-to-all | bytes 524288 | tf_op jit(solution)/shard_map/all_to_all | solution.py:98
  397.2 63.1 %psum.31 = f32[]{:T(128)} all-reduce(f32[]{:T(128)} %multiply_reduce_fusion), channel_id=1, replica_groups=mesh['px'=8,'py'=16] {'px','py'}, use_global_device_ids=true, to_apply=%region_14.15 | all-reduce | flops 1 | bytes 8 | tf_op jit(solution)/shard_map/psum | solution.py:58
  (169 shorter events, 63.1 us)
Async XLA Ops:
  0.6 23.3 %copy-start = (f32[2,1,128,256]{3,2,1,0:T(8,128)S(1)}, f32[2,1,128,256]{3,2,1,0:T(8,128)}, u32[]{:S(2)}) copy-start(f32[2,1,128,256]{3,2,1,0:T(8,128)} %param.13) | copy-start | bytes 786436
  13.5 16.6 %all-to-all-start = ((s32[16,192,1]{1,2,0:T(1,128)}), s32[16,192,1]{1,2,0:T(1,128)S(1)}, u32[]{:S(2)}, u32[]{:S(2)}) async-start(s32[16,192,1]{1,2,0:T(1,128)} %all_to_all.143), calls=%async_computation | async-start | bytes 32768 | tf_op jit(solution)/shard_map/all_to_all | solution.py:86
  23.9 0.9 copy-start.6
  30.0 17.1 %all-to-all-start.1 = ((f32[16,192,1]{1,2,0:T(1,128)}), f32[16,192,1]{1,2,0:T(1,128)S(1)}, u32[]{:S(2)}, u32[]{:S(2)}) async-start(f32[16,192,1]{1,2,0:T(1,128)} %all_to_all.144), calls=%async_computation.1 | async-start | bytes 32768 | tf_op jit(solution)/shard_map/all_to_all | solution.py:85
  47.2 12.5 %all-to-all-start.4 = ((f32[2,1,128,256]{3,0,1,2:T(2,128)}), f32[2,1,128,256]{3,0,1,2:T(2,128)S(1)}, u32[]{:S(2)}, u32[]{:S(2)}) async-start(f32[2,1,128,256]{3,0,1,2:T(2,128)} %copy.120), calls=%async_computation.4 | async-start | bytes 524288 | tf_op jit(solution)/shard_map/all_to_all | solution.py:92
  59.6 27.5 %all-to-all-start.2 = ((f32[16,192,128]{2,1,0:T(8,128)}), f32[16,192,128]{2,1,0:T(8,128)S(1)}, u32[]{:S(2)}, u32[]{:S(2)}) async-start(f32[16,192,128]{2,1,0:T(8,128)} %bitcast.7), calls=%async_computation.2 | async-start | bytes 3145728 | tf_op jit(solution)/shard_map/all_to_all | solution.py:84
  87.1 23.8 %copy-start.3 = (f32[16,192,128]{2,1,0:T(8,128)}, f32[16,192,128]{2,1,0:T(8,128)S(1)}, u32[]{:S(2)}) copy-start(f32[16,192,128]{2,1,0:T(8,128)S(1)} %all-to-all-done.2) | copy-start | bytes 4718596
  87.1 23.8 %all-to-all-start.3 = ((f32[16,192,128]{2,1,0:T(8,128)}), f32[16,192,128]{2,1,0:T(8,128)}, u32[]{:S(2)}, u32[]{:S(2)}) async-start(f32[16,192,128]{2,1,0:T(8,128)} %bitcast.9), calls=%async_computation.3 | async-start | bytes 3145728 | tf_op jit(solution)/shard_map/all_to_all | solution.py:83
  168.9 1.4 copy-start.4
  277.7 63.8 %copy-start.1 = (f32[2,1,128,256]{3,2,0,1:T(8,128)}, f32[2,1,128,256]{3,2,0,1:T(8,128)S(1)}, u32[]{:S(2)}) copy-start(f32[2,1,128,256]{3,2,0,1:T(8,128)S(1)} %get-tuple-element.39) | copy-start | bytes 786436
  353.7 1.4 copy-start.5
  396.3 65.3 %copy-start.2 = (f32[2,1,128,256]{3,2,0,1:T(8,128)S(1)}, f32[2,1,128,256]{3,2,0,1:T(8,128)}, u32[]{:S(2)}) copy-start(f32[2,1,128,256]{3,2,0,1:T(8,128)} %copy-done.1) | copy-start | bytes 786436
where the time goes:
time: 471 us; the launch traced here: 463 us
  blocking collectives  244 us (52%)
  matrix products  63.2 us (13%)
  local copies, waits for them, and re-layouts  47.9 us (10%)
  waiting for transfers between devices  44.8 us (10%)
  starting transfers between devices  32.7 us (7%)
  other arithmetic  24.5 us (5%)
  between operations  5.82 us (1%)
    psum x3, blocking collectives, dot_total(): return lax.psum(jnp.sum(left_side * right_side), ('px', 'py'))  189 us
    dot_general x3, matrix products, misfit(): lax.dot_general(interp_matrix, weighted, (((0,), (0,)), ((), ())), precis...  35.4 us
    all_to_all x3, blocking collectives, adjoint(): lax.all_to_all(diffuse(values_in, coef_y, 3), 'px', split_axis=3, concat_...  34.3 us
    dot_general x3, matrix products, misfit(): jnp.dot(interp_matrix, flat_field, precision=lax.Precision.HIGHEST, prefe...  27.7 us
    all_to_all x2, blocking collectives, forward(): lax.all_to_all(diffuse(values_in, coef_x, 2), 'px', split_axis=2, concat_...  20.9 us
    all_to_all x1, waiting for transfers between devices, shards(): lax.all_to_all(bucket(obs_weight), 'py', split_axis=0, concat_axis=0, til...  19.9 us
    unnamed x20, local copies, waits for them, and re-layouts  19.2 us
    all_to_all x1, waiting for transfers between devices, shards(): lax.all_to_all(bucket(innovation), 'py', split_axis=0, concat_axis=0, til...  18.5 us
  transfers between devices with their start and end apart: 5, of which 3 were waited for; matrix products, arithmetic and copies ran while one was open for 4% of the time, Pallas kernels for 0%

commit v1 on v0

--- a/solution.py
+++ b/solution.py
@@ -89,9 +89,10 @@
     interp_matrix = build_interp(shares_in, rows_in, F * LZ * LX * NB)
 
     def forward(values_in):
-        turned = lax.all_to_all(
-            diffuse(values_in, coef_x, 2), "px", split_axis=2, concat_axis=3, tiled=True
-        )
+        block = diffuse(values_in, coef_x, 2)
+        parts = jnp.split(block, lax.axis_size("px"), axis=2)
+        received = lax.all_to_all(jnp.stack(parts), "px", 0, 0)
+        turned = jnp.concatenate(received, axis=3)
         return diffuse(turned, coef_y, 3)
 
     def adjoint(values_in):

time: 471 us -> 474 us (level)
    unnamed x20 -> x41, local copies, waits for them, and re-layouts: 19.2 us -> 23 us
  transfers between devices with their start and end apart: 5 -> 5, of which waited for: 3 -> 3; matrix products, arithmetic and copies ran while one was open for 4% -> 5% of each run, Pallas kernels for 0% -> 0%
where the time goes in v1:
time: 474 us; the launch traced here: 466 us
  blocking collectives  244 us (51%)
  matrix products  63.1 us (13%)
  local copies, waits for them, and re-layouts  50.9 us (11%)
  waiting for transfers between devices  44.9 us (9%)
  starting transfers between devices  32.7 us (7%)
  other arithmetic  24.5 us (5%)
  between operations  5.92 us (1%)
    psum x3, blocking collectives, dot_total(): return lax.psum(jnp.sum(left_side * right_side), ('px', 'py'))  189 us
    dot_general x3, matrix products, misfit(): lax.dot_general(interp_matrix, weighted, (((0,), (0,)), ((), ())), precis...  35.4 us
    all_to_all x3, blocking collectives, adjoint(): lax.all_to_all(diffuse(values_in, coef_y, 3), 'px', split_axis=3, concat_...  34.3 us
    dot_general x3, matrix products, misfit(): jnp.dot(interp_matrix, flat_field, precision=lax.Precision.HIGHEST, prefe...  27.7 us
    unnamed x41, local copies, waits for them, and re-layouts  23 us
    all_to_all x2, blocking collectives, forward(): received = lax.all_to_all(jnp.stack(parts), 'px', 0, 0)  20.9 us
    all_to_all x1, waiting for transfers between devices, shards(): lax.all_to_all(bucket(obs_weight), 'py', split_axis=0, concat_axis=0, til...  19.9 us
    all_to_all x1, waiting for transfers between devices, shards(): lax.all_to_all(bucket(innovation), 'py', split_axis=0, concat_axis=0, til...  18.5 us
  transfers between devices with their start and end apart: 5, of which 3 were waited for; matrix products, arithmetic and copies ran while one was open for 5% of the time, Pallas kernels for 0%

profile of v1, /device:TPU:1, one launch (start us, length us, event | category | flops | bytes accessed | tf_op | source)
XLA Modules:
  0.0 465.9 jit_solution(7660563149025196484)
XLA Ops:
  13.4 8.4 %all-to-all-start = ((s32[16,192,1]{1,2,0:T(1,128)}), s32[16,192,1]{1,2,0:T(1,128)S(1)}, u32[]{:S(2)}, u32[]{:S(2)}) async-start(s32[16,192,1]{1,2,0:T(1,128)} %all_to_all.104), calls=%async_computation | async-start | bytes 32768 | tf_op jit(solution)/shard_map/all_to_all | solution.py:86
  33.8 6.7 %all-to-all-start.1 = ((f32[16,192,1]{1,2,0:T(1,128)}), f32[16,192,1]{1,2,0:T(1,128)S(1)}, u32[]{:S(2)}, u32[]{:S(2)}) async-start(f32[16,192,1]{1,2,0:T(1,128)} %all_to_all.105), calls=%async_computation.1 | async-start | bytes 32768 | tf_op jit(solution)/shard_map/all_to_all | solution.py:85
  41.0 4.7 %scatter_custom_fusion.2 = f32[3072,128]{1,0:T(8,128)} fusion(s32[1024]{0:T(1024)S(1)} %bitcast.248, f32[1024,128]{1,0:T(8,128)} %param.17, f32[]{:T(128)} %constant.119.clone.1), kind=kCustom, calls=%fused_computation.51 | custom fusion | bytes 1573376 | tf_op jit(solution)/shard_map/scatter | solution.py:80
  45.7 4.7 %scatter_custom_fusion.3 = f32[3072,128]{1,0:T(8,128)} fusion(s32[1024]{0:T(1024)S(1)} %bitcast.249, f32[1024,128]{1,0:T(8,128)} %param.16, f32[]{:T(128)} %constant.119.clone.1), kind=kCustom, calls=%fused_computation.49 | custom fusion | bytes 1573376 | tf_op jit(solution)/shard_map/scatter | solution.py:80
  50.5 6.0 %all-to-all-start.4 = ((f32[8,2,1,16,256]{4,3,1,2,0:T(8,128)}), f32[8,2,1,16,256]{4,3,1,2,0:T(8,128)S(1)}, u32[]{:S(2)}, u32[]{:S(2)}) async-start(f32[8,2,1,16,256]{4,3,1,2,0:T(8,128)} %constant_dynamic-update-slice_fusion), calls=%async_computation.4 | async-start | bytes 524288 | tf_op jit(solution)/shard_map/all_to_all | solution.py:94
  56.6 6.4 %all-to-all-done.4 = f32[8,2,1,16,256]{4,3,1,2,0:T(8,128)S(1)} async-done(((f32[8,2,1,16,256]{4,3,1,2,0:T(8,128)}), f32[8,2,1,16,256]{4,3,1,2,0:T(8,128)S(1)}, u32[]{:S(2)}, u32[]{:S(2)}) %all-to-all-start.4) | async-done | bytes 262176 | tf_op jit(solution)/shard_map/all_to_all | solution.py:94
  63.0 6.9 %all-to-all-start.2 = ((f32[16,192,128]{2,1,0:T(8,128)}), f32[16,192,128]{2,1,0:T(8,128)S(1)}, u32[]{:S(2)}, u32[]{:S(2)}) async-start(f32[16,192,128]{2,1,0:T(8,128)} %bitcast.6), calls=%async_computation.2 | async-start | bytes 3145728 | tf_op jit(solution)/shard_map/all_to_all | solution.py:84
  70.5 19.9 %all-to-all-done.2 = f32[16,192,128]{2,1,0:T(8,128)S(1)} async-done(((f32[16,192,128]{2,1,0:T(8,128)}), f32[16,192,128]{2,1,0:T(8,128)S(1)}, u32[]{:S(2)}, u32[]{:S(2)}) %all-to-all-start.2) | async-done | bytes 1572896 | tf_op jit(solution)/shard_map/all_to_all | solution.py:84
  90.5 4.7 %all-to-all-start.3 = ((f32[16,192,128]{2,1,0:T(8,128)}), f32[16,192,128]{2,1,0:T(8,128)}, u32[]{:S(2)}, u32[]{:S(2)}) async-start(f32[16,192,128]{2,1,0:T(8,128)} %bitcast.8), calls=%async_computation.3 | async-start | bytes 3145728 | tf_op jit(solution)/shard_map/all_to_all | solution.py:83
  95.8 18.5 %all-to-all-done.3 = f32[16,192,128]{2,1,0:T(8,128)} async-done(((f32[16,192,128]{2,1,0:T(8,128)}), f32[16,192,128]{2,1,0:T(8,128)}, u32[]{:S(2)}, u32[]{:S(2)}) %all-to-all-start.3) | async-done | bytes 1572896 | tf_op jit(solution)/shard_map/all_to_all | solution.py:83
  114.3 9.5 %fusion.11 = f32[3072,128]{1,0:T(8,128)S(1)} fusion(f32[3072,128]{1,0:T(8,128)S(1)} %bitcast.212, f32[3072,128]{1,0:T(8,128)} %bitcast.9, f32[512,128]{1,0:T(8,128)S(1)} %reshape.143, f32[3072]{0:T(1024)S(1)} %all_to_all.82, s32[3072]{0:T(1024)S(1)} %broadcast_add_fusion.1, f32[3072]{0:T(1024)S(1)} %broadcast_subtract_fusion, s32[3072]{0:T(1024)S(1)} %eq.64), kind=kOutput, calls=%fused_computation.18 | convolution fusion | flops 2424569856 | bytes 5029888 | tf_op jit(solution)/shard_map/dot_general | solution.py:40
  123.9 11.8 %fusion.4 = f32[512,128]{1,0:T(8,128)S(1)} fusion(f32[3072,128]{1,0:T(8,128)S(1)} %fusion.11, f32[3072]{0:T(1024)S(1)} %all_to_all.82, s32[3072]{0:T(1024)S(1)} %broadcast_add_fusion.1, f32[3072]{0:T(1024)S(1)} %broadcast_subtract_fusion, s32[3072]{0:T(1024)S(1)} %eq.64), kind=kOutput, calls=%fused_computation.10 | convolution fusion | flops 2423783424 | bytes 1884160 | tf_op jit(solution)/shard_map/dot_general | solution.py:47
  140.9 14.4 %all_to_all.116 = f32[8,1,8192]{2,1,0:T(1,128)S(1)} all-to-all(f32[8,1,8192]{2,1,0:T(1,128)S(1)} %reshape.195), channel_id=1, replica_groups=mesh['px'=8,'py'=16] {'px'}, dimensions={0} | all-to-all | bytes 524288 | tf_op jit(solution)/shard_map/all_to_all | solution.py:99
  161.6 9.9 %all_to_all.117 = f32[8,2,1,16,256]{4,3,1,2,0:T(8,128)S(1)} all-to-all(f32[8,2,1,16,256]{4,3,1,2,0:T(8,128)S(1)} %constant_dynamic-update-slice_fusion.8), channel_id=1, replica_groups=mesh['px'=8,'py'=16] {'px'}, dimensions={0} | all-to-all | bytes 524288 | tf_op jit(solution)/shard_map/all_to_all | solution.py:94
  173.6 9.1 %fusion.10 = f32[3072,128]{1,0:T(8,128)S(1)} fusion(f32[3072,128]{1,0:T(8,128)S(1)} %bitcast.213, f32[512,128]{1,0:T(8,128)S(1)} %reshape.147, f32[3072]{0:T(1024)S(1)} %all_to_all.82, s32[3072]{0:T(1024)S(1)} %broadcast_add_fusion.1, f32[3072]{0:T(1024)S(1)} %broadcast_subtract_fusion, s32[3072]{0:T(1024)S(1)} %eq.64), kind=kOutput, calls=%fused_computation.17 | convolution fusion | flops 2424569856 | bytes 3457024 | tf_op jit(solution)/shard_map/dot_general | solution.py:40
  182.7 11.8 %fusion.2 = f32[512,128]{1,0:T(8,128)S(1)} fusion(f32[3072,128]{1,0:T(8,128)S(1)} %fusion.10, f32[3072]{0:T(1024)S(1)} %all_to_all.82, s32[3072]{0:T(1024)S(1)} %broadcast_add_fusion.1, f32[3072]{0:T(1024)S(1)} %broadcast_subtract_fusion, s32[3072]{0:T(1024)S(1)} %eq.64), kind=kOutput, calls=%fused_computation.8 | convolution fusion | flops 2423783424 | bytes 1884160 | tf_op jit(solution)/shard_map/dot_general | solution.py:47
  200.0 9.9 %all_to_all.118 = f32[8,1,8192]{2,1,0:T(1,128)S(1)} all-to-all(f32[8,1,8192]{2,1,0:T(1,128)S(1)} %reshape.197), channel_id=1, replica_groups=mesh['px'=8,'py'=16] {'px'}, dimensions={0} | all-to-all | bytes 524288 | tf_op jit(solution)/shard_map/all_to_all | solution.py:99
  216.0 63.0 %all-reduce.96 = (f32[]{:T(128)}, f32[]{:T(128)}) all-reduce(f32[]{:T(128)} %get-tuple-element.27, f32[]{:T(128)} %get-tuple-element.26), channel_id=1, replica_groups=mesh['px'=8,'py'=16] {'px','py'}, use_global_device_ids=true, to_apply=%region_8.9 | all-reduce | flops 2 | bytes 16 | tf_op jit(solution)/shard_map/psum | solution.py:58
  281.0 62.5 %psum.30 = f32[]{:T(128)} all-reduce(f32[]{:T(128)} %get-tuple-element.30), channel_id=1, replica_groups=mesh['px'=8,'py'=16] {'px','py'}, use_global_device_ids=true, to_apply=%region_12.13 | all-reduce | flops 1 | bytes 8 | tf_op jit(solution)/shard_map/psum | solution.py:58
  345.3 11.0 %all_to_all.119 = f32[8,2,1,16,256]{4,3,1,2,0:T(8,128)S(1)} all-to-all(f32[8,2,1,16,256]{4,3,1,2,0:T(8,128)S(1)} %constant_dynamic-update-slice_fusion.16), channel_id=1, replica_groups=mesh['px'=8,'py'=16] {'px'}, dimensions={0} | all-to-all | bytes 524288 | tf_op jit(solution)/shard_map/all_to_all | solution.py:94
  358.2 9.1 %fusion.9 = f32[3072,128]{1,0:T(8,128)S(1)} fusion(f32[3072,128]{1,0:T(8,128)S(1)} %bitcast.214, f32[512,128]{1,0:T(8,128)S(1)} %reshape.151, f32[3072]{0:T(1024)S(1)} %all_to_all.82, s32[3072]{0:T(1024)S(1)} %broadcast_add_fusion.1, f32[3072]{0:T(1024)S(1)} %broadcast_subtract_fusion, s32[3072]{0:T(1024)S(1)} %eq.64), kind=kOutput, calls=%fused_computation.16 | convolution fusion | flops 2424569856 | bytes 3457024 | tf_op jit(solution)/shard_map/dot_general | solution.py:40
  367.3 11.8 %fusion = f32[512,128]{1,0:T(8,128)S(1)} fusion(f32[3072,128]{1,0:T(8,128)S(1)} %fusion.9, f32[3072]{0:T(1024)S(1)} %all_to_all.82, s32[3072]{0:T(1024)S(1)} %broadcast_add_fusion.1, f32[3072]{0:T(1024)S(1)} %broadcast_subtract_fusion, s32[3072]{0:T(1024)S(1)} %eq.64), kind=kOutput, calls=%fused_computation.6 | convolution fusion | flops 2423783424 | bytes 1884160 | tf_op jit(solution)/shard_map/dot_general | solution.py:47
  384.4 9.9 %all_to_all.120 = f32[8,1,8192]{2,1,0:T(1,128)S(1)} all-to-all(f32[8,1,8192]{2,1,0:T(1,128)S(1)} %reshape.199), channel_id=1, replica_groups=mesh['px'=8,'py'=16] {'px'}, dimensions={0} | all-to-all | bytes 524288 | tf_op jit(solution)/shard_map/all_to_all | solution.py:99
  400.3 63.1 %psum.31 = f32[]{:T(128)} all-reduce(f32[]{:T(128)} %multiply_reduce_fusion), channel_id=1, replica_groups=mesh['px'=8,'py'=16] {'px','py'}, use_global_device_ids=true, to_apply=%region_14.15 | all-reduce | flops 1 | bytes 8 | tf_op jit(solution)/shard_map/psum | solution.py:58
  (187 shorter events, 66.1 us)
Async XLA Ops:
  0.6 23.2 %copy-start = (f32[2,1,128,256]{3,2,1,0:T(8,128)S(1)}, f32[2,1,128,256]{3,2,1,0:T(8,128)}, u32[]{:S(2)}) copy-start(f32[2,1,128,256]{3,2,1,0:T(8,128)} %param.13) | copy-start | bytes 786436
  13.4 20.3 %all-to-all-start = ((s32[16,192,1]{1,2,0:T(1,128)}), s32[16,192,1]{1,2,0:T(1,128)S(1)}, u32[]{:S(2)}, u32[]{:S(2)}) async-start(s32[16,192,1]{1,2,0:T(1,128)} %all_to_all.104), calls=%async_computation | async-start | bytes 32768 | tf_op jit(solution)/shard_map/all_to_all | solution.py:86
  24.0 3.9 copy-start.6
  33.8 16.8 %all-to-all-start.1 = ((f32[16,192,1]{1,2,0:T(1,128)}), f32[16,192,1]{1,2,0:T(1,128)S(1)}, u32[]{:S(2)}, u32[]{:S(2)}) async-start(f32[16,192,1]{1,2,0:T(1,128)} %all_to_all.105), calls=%async_computation.1 | async-start | bytes 32768 | tf_op jit(solution)/shard_map/all_to_all | solution.py:85
  50.5 12.5 %all-to-all-start.4 = ((f32[8,2,1,16,256]{4,3,1,2,0:T(8,128)}), f32[8,2,1,16,256]{4,3,1,2,0:T(8,128)S(1)}, u32[]{:S(2)}, u32[]{:S(2)}) async-start(f32[8,2,1,16,256]{4,3,1,2,0:T(8,128)} %constant_dynamic-update-slice_fusion), calls=%async_computation.4 | async-start | bytes 524288 | tf_op jit(solution)/shard_map/all_to_all | solution.py:94
  63.0 27.5 %all-to-all-start.2 = ((f32[16,192,128]{2,1,0:T(8,128)}), f32[16,192,128]{2,1,0:T(8,128)S(1)}, u32[]{:S(2)}, u32[]{:S(2)}) async-start(f32[16,192,128]{2,1,0:T(8,128)} %bitcast.6), calls=%async_computation.2 | async-start | bytes 3145728 | tf_op jit(solution)/shard_map/all_to_all | solution.py:84
  90.5 23.8 %copy-start.3 = (f32[16,192,128]{2,1,0:T(8,128)}, f32[16,192,128]{2,1,0:T(8,128)S(1)}, u32[]{:S(2)}) copy-start(f32[16,192,128]{2,1,0:T(8,128)S(1)} %all-to-all-done.2) | copy-start | bytes 4718596
  90.5 23.8 %all-to-all-start.3 = ((f32[16,192,128]{2,1,0:T(8,128)}), f32[16,192,128]{2,1,0:T(8,128)}, u32[]{:S(2)}, u32[]{:S(2)}) async-start(f32[16,192,128]{2,1,0:T(8,128)} %bitcast.8), calls=%async_computation.3 | async-start | bytes 3145728 | tf_op jit(solution)/shard_map/all_to_all | solution.py:83
  172.2 1.4 copy-start.4
  281.0 63.8 %copy-start.1 = (f32[2,1,128,256]{3,2,1,0:T(8,128)}, f32[2,1,128,256]{3,2,1,0:T(8,128)S(1)}, u32[]{:S(2)}) copy-start(f32[2,1,128,256]{3,2,1,0:T(8,128)S(1)} %get-tuple-element.31) | copy-start | bytes 786436
  356.8 1.4 copy-start.5
  399.4 65.3 %copy-start.2 = (f32[2,1,128,256]{3,2,1,0:T(8,128)S(1)}, f32[2,1,128,256]{3,2,1,0:T(8,128)}, u32[]{:S(2)}) copy-start(f32[2,1,128,256]{3,2,1,0:T(8,128)} %copy-done.1) | copy-start | bytes 786436
